TPU v7x, 32 devices: a whole 2x2x4 slice. The times are simulated.
32 devices in a mesh: row: 4 (over z), col: 8 (over y, x, core).
Axes of the slice: x: 2, y: 2, z: 4, core: 2. Of those that a mesh axis runs over, the one named last changes fastest.
Arguments:
- velocity: bfloat16 [3, 8, 2048, 2048], P(None, 'col', 'row'), may hold values from -6 to 6
- vorticity: bfloat16 [3, 8, 2048, 2048], P(None, 'col', 'row'), may hold values from -6 to 6
- eddy_state: bfloat16 [8, 64, 3072], P('col', 'row'), may hold values from -0.359375 to 0.359375
- eddy_rate: bfloat16 [8, 64], P('col', 'row'), may hold values from 8 to 64
- block_owner: int32 [8, 4, 64, 1], P('col', 'row'), may hold values from 0 to 3; in each aligned block of 64 rows (0 to 63, 64 to 127, ..., all dimensions but the last counted through in order) at most 32 rows name the same one
- block_slot: int32 [8, 4, 64], P('col', 'row'), may hold values from 0 to 15
Outputs:
- spectral: float32 [3, 8, 1638400], P(None, None, ('row', 'col'))
Inputs may be any that keep to these rules, and one draw needn't show every extreme that they name: `block_owner`: among the 64 blocks of one DNS device, at most 32 have the same owner.
All inputs are finite; a program needn't handle non-finite values.
Results may differ from a plain program's by a relative error of at most 0.013.
Values may be sent and summed in bfloat16 or wider, within the bound.
A program may use at most 128 MiB of HBM per device.

v0:
```python
import math
import jax
import jax.numpy as jnp
from jax import lax
from jax.sharding import PartitionSpec as P

NX = 2048
NY = 2048
KXM = 640
KYM = 1280
RATIO = 4
BY = 8
BX = 128
S = 16
BLKV = 3072
section_step = 0.5
viscous_step = 0.15
vertical_step = 0.5


def padded_2(cells, sides, width):
    for axis, dim in sides:
        count = lax.axis_size(axis)
        head = lax.slice_in_dim(cells, 0, width, axis=dim)
        tail = lax.slice_in_dim(cells, cells.shape[dim] - width, cells.shape[dim], axis=dim)
        cells = jnp.concatenate(
            [
                lax.ppermute(tail, axis, [(i, (i + 1) % count) for i in range(count)]),
                cells,
                lax.ppermute(head, axis, [((i + 1) % count, i) for i in range(count)]),
            ],
            axis=dim,
        )
    return cells


def gauss_value(position, ratio):
    spread = 4.0 * ratio * ratio
    taps = jnp.arange(5 * ratio).astype(jnp.float32)
    shifted = taps - 2.0 * ratio - (ratio - 1) / 2.0
    total = jnp.sum(jnp.exp(-shifted * shifted / (2.0 * spread)))
    moved = position - 2.0 * ratio - (ratio - 1) / 2.0
    return jnp.exp(-moved * moved / (2.0 * spread)) / total


def x_weights(points, coarse, ratio):
    fine = jnp.arange(points, dtype=jnp.int32)[:, None]
    cells = jnp.arange(coarse, dtype=jnp.int32)[None, :]
    offset = jnp.mod(fine - ratio * cells + 2 * ratio, points)
    value = gauss_value(offset.astype(jnp.float32), ratio)
    return jnp.where(offset < 5 * ratio, value, 0.0).astype(jnp.bfloat16)


def y_weights(coarse, padded, ratio):
    cells = jnp.arange(coarse, dtype=jnp.int32)[:, None]
    fine = jnp.arange(padded, dtype=jnp.int32)[None, :]
    offset = fine - ratio * cells
    value = gauss_value(offset.astype(jnp.float32), ratio)
    return jnp.where((offset >= 0) & (offset < 5 * ratio), value, 0.0).astype(jnp.bfloat16)


def x_table(points, kept):
    fine = jnp.arange(points, dtype=jnp.int32)[:, None]
    column = jnp.arange(2 * kept, dtype=jnp.int32)[None, :]
    phase = jnp.mod(column // 2 * fine, points).astype(jnp.float32) * (2.0 * math.pi / points)
    value = jnp.where(column % 2 == 0, jnp.cos(phase), -jnp.sin(phase))
    return (value / math.sqrt(points)).astype(jnp.bfloat16)


def y_tables(points, kept, first, count):
    fine = jnp.arange(points, dtype=jnp.int32)[:, None]
    wave = jnp.arange(count, dtype=jnp.int32)[None, :] + (first - kept // 2)
    phase = jnp.mod(wave * fine, points).astype(jnp.float32) * (2.0 * math.pi / points)
    scale = 1.0 / math.sqrt(points)
    return (
        (jnp.cos(phase) * scale).astype(jnp.bfloat16),
        (jnp.sin(phase) * scale).astype(jnp.bfloat16),
    )


def vertical_inverse(planes):
    index = jnp.arange(planes)
    ends = (index == 0) | (index == planes - 1)
    diagonal = jnp.where(ends, 1.0 + vertical_step, 1.0 + 2.0 * vertical_step).astype(jnp.float32)
    lower = jnp.where(index == 0, 0.0, -vertical_step).astype(jnp.float32)
    upper = jnp.where(index == planes - 1, 0.0, -vertical_step).astype(jnp.float32)
    return lax.linalg.tridiagonal_solve(lower, diagonal, upper, jnp.eye(planes, dtype=jnp.float32))


def damping(x_wave, y_wave, points_x, points_y):
    angle_x = x_wave.astype(jnp.float32) * (2.0 * math.pi / points_x)
    angle_y = y_wave.astype(jnp.float32) * (2.0 * math.pi / points_y)
    total = (
        angle_y[:, None, None] * angle_y[:, None, None]
        + angle_x[None, None, :] * angle_x[None, None, :]
    )
    return jnp.broadcast_to(jnp.exp(-viscous_step * total), (y_wave.shape[0], 2, x_wave.shape[0]))


def along_y(piece):
    items, width, length = piece.shape
    half = width // 2
    split = piece.reshape(items, half, 2, length)
    real_in = split[:, :, 0, :]
    imag_in = split[:, :, 1, :]
    block = 256
    outputs = []
    for first in range(0, KYM, block):
        cosine, sine = y_tables(length, KYM, first, block)
        real_out = jnp.einsum(
            "kin,nj->kji", real_in, cosine, preferred_element_type=jnp.float32
        ) + jnp.einsum("kin,nj->kji", imag_in, sine, preferred_element_type=jnp.float32)
        imag_out = jnp.einsum(
            "kin,nj->kji", imag_in, cosine, preferred_element_type=jnp.float32
        ) - jnp.einsum("kin,nj->kji", real_in, sine, preferred_element_type=jnp.float32)
        outputs.append(jnp.concatenate([real_out, imag_out], axis=2))
    return jnp.concatenate(outputs, axis=1).astype(jnp.bfloat16)


def per_device(velocity, vorticity, eddy_state, eddy_rate, block_owner, block_slot):
    components, depth, rows, points = velocity.shape
    coarse_rows = rows // RATIO
    coarse_cols = points // RATIO
    xweights = x_weights(points, coarse_cols, RATIO)
    local = jnp.einsum(
        "czyn,nx->czyx", velocity, xweights, preferred_element_type=jnp.float32
    ).astype(jnp.bfloat16)
    along = padded_2(local, (("row", 2),), 2 * RATIO)
    yweights = y_weights(coarse_rows, rows + 4 * RATIO, RATIO)
    filtered = jnp.einsum(
        "iy,czyx->czix", yweights, along, preferred_element_type=jnp.float32
    ).astype(jnp.bfloat16)
    ybands = coarse_rows // BY
    xbands = coarse_cols // BX
    count = depth * ybands * xbands
    blocks = filtered.reshape(components, depth, ybands, BY, xbands, BX).transpose(1, 2, 4, 0, 3, 5)
    blocks = blocks.reshape(count, BLKV)
    owners = block_owner.reshape(count)
    slots = block_slot.reshape(count)
    owners_total = lax.axis_size("row")
    every_state, every_rate = (
        lax.all_gather(eddy_state, "row", axis=1, tiled=True),
        lax.all_gather(eddy_rate, "row", axis=1, tiled=True),
    )
    chosen = owners * S + slots
    lookup = (chosen[:, None] == jnp.arange(owners_total * S, dtype=jnp.int32)[None, :]).astype(
        jnp.bfloat16
    )
    state = jnp.dot(lookup, every_state[0], preferred_element_type=jnp.float32)
    rates = jnp.dot(lookup, every_rate[0][:, None], preferred_element_type=jnp.float32)[:, 0]
    forcing_blocks = (rates[:, None] * (state - blocks.astype(jnp.float32))).astype(jnp.bfloat16)
    coarse = forcing_blocks.reshape(depth, ybands, xbands, components, BY, BX).transpose(
        3, 0, 1, 4, 2, 5
    )
    coarse = coarse.reshape(components, depth, coarse_rows, coarse_cols).astype(jnp.float32)
    forcing = jnp.repeat(jnp.repeat(coarse, RATIO, axis=2), RATIO, axis=3)
    speed = velocity.astype(jnp.float32)
    spin = vorticity.astype(jnp.float32)
    cross = jnp.stack(
        [
            speed[1] * spin[2] - speed[2] * spin[1],
            speed[2] * spin[0] - speed[0] * spin[2],
            speed[0] * spin[1] - speed[1] * spin[0],
        ],
        axis=0,
    )
    section = (speed + section_step * (cross + forcing)).astype(jnp.bfloat16)
    xtable = x_table(points, KXM)
    spectrum = jnp.einsum(
        "kyn,nm->kmy",
        section.reshape(components * depth, rows, points),
        xtable,
        preferred_element_type=jnp.float32,
    ).astype(jnp.bfloat16)
    ordered = along_y(lax.all_to_all(spectrum, "row", split_axis=1, concat_axis=2, tiled=True))
    ordered = ordered.reshape(components, depth, KYM, -1)
    inverse = vertical_inverse(depth * lax.axis_size("col")).astype(jnp.bfloat16)
    mode_rows = KYM // lax.axis_size("col")
    mode_cols = ordered.shape[3] // 2
    x_wave = lax.axis_index("row") * mode_cols + jnp.arange(mode_cols, dtype=jnp.int32)
    y_wave = lax.axis_index("col") * mode_rows + jnp.arange(mode_rows, dtype=jnp.int32) - KYM // 2
    factor = damping(x_wave, y_wave, NX, NY).reshape(-1)
    piece = lax.all_to_all(ordered, "col", split_axis=2, concat_axis=1, tiled=True)
    items = piece.shape[0]
    flat = piece.reshape(items, piece.shape[1], -1)
    mixed = jnp.einsum("wz,kzl->kwl", inverse, flat, preferred_element_type=jnp.float32)
    return mixed * factor[None, None, :]


def solution(mesh):
    return jax.shard_map(
        per_device,
        mesh=mesh,
        in_specs=(
            P(None, "col", "row", None),
            P(None, "col", "row", None),
            P("col", "row", None),
            P("col", "row"),
            P("col", "row", None, None),
            P("col", "row", None),
        ),
        out_specs=P(None, None, ("row", "col")),
        check_vma=False,
    )
```

profile of v0, /device:TPU:0, one launch (start us, length us, event | category | flops | bytes accessed | tf_op | source)
XLA Modules:
  0.0 582.2 jit_solution(14752560193493699065)
XLA Ops:
  13.9 8.7 %copy.30 = bf16[3,1,512,2048]{2,3,0,1:T(8,128)(2,1)} copy(bf16[3,1,512,2048]{3,2,1,0:T(8,128)(2,1)} %param.6) | data formatting | bytes 12582912 | tf_op args[0]
  24.1 10.3 %all-reduce = bf16[64]{0:T(256)(128)(2,1)S(1)} all-reduce(bf16[64]{0:T(256)(128)(2,1)S(1)} %dynamic-update-slice), channel_id=1, replica_groups=mesh['row'=4,'col'=8] {'row'}, use_global_device_ids=true, to_apply=%add | all-reduce | flops 64 | bytes 256 | tf_op jit(solution)/shard_map/reshape
  34.4 14.6 %all_gather.7 = bf16[1,64,3072]{2,1,0:T(8,128)(2,1)S(1)} all-gather(bf16[1,16,3072]{2,1,0:T(8,128)(2,1)S(1)} %copy-done.1), channel_id=1, replica_groups=mesh['row'=4,'col'=8] {'row'}, dimensions={1}, use_global_device_ids=true | all-gather | bytes 491520 | tf_op jit(solution)/shard_map/all_gather | solution.py:142
  49.1 9.2 %convert_element_type.226 = f32[3,1,512,2048]{2,3,0,1:T(8,128)} convert(bf16[3,1,512,2048]{2,3,0,1:T(8,128)(2,1)} %copy.30) | non-fusion elementwise | flops 3145728 | bytes 18874368 | tf_op jit(solution)/shard_map/convert_element_type | solution.py:157
  58.3 8.6 %copy.31 = bf16[3,1,512,2048]{2,3,0,1:T(8,128)(2,1)} copy(bf16[3,1,512,2048]{3,2,1,0:T(8,128)(2,1)} %param.7) | data formatting | bytes 12582912 | tf_op args[1]
  66.8 9.7 %convert_element_type.227 = f32[3,1,512,2048]{2,3,0,1:T(8,128)} convert(bf16[3,1,512,2048]{2,3,0,1:T(8,128)(2,1)} %copy.31) | non-fusion elementwise | flops 3145728 | bytes 18874368 | tf_op jit(solution)/shard_map/convert_element_type | solution.py:158
  76.7 10.0 %multiply_subtract_fusion.2 = (f32[1,1,512,2048]{2,3,0,1:T(8,128)}, f32[1,1,512,2048]{2,3,0,1:T(8,128)}, f32[1,1,512,2048]{2,3,0,1:T(8,128)}) fusion(f32[3,1,512,2048]{2,3,0,1:T(8,128)} %convert_element_type.227, f32[3,1,512,2048]{2,3,0,1:T(8,128)S(1)} %copy-done), kind=kLoop, calls=%fused_computation.41 | loop fusion | flops 9437184 | bytes 37748736 | tf_op jit(solution)/shard_map/sub | solution.py:161
  86.8 45.1 %fusion.364 = bf16[2048,1280,1]{0,1,2:T(8,128)(2,1)} fusion(s32[1280]{0:T(1024)S(1)} %add_select_fusion.7, pred[1280]{0:T(1024)(128)(4,1)S(1)} %fusion.192), kind=kLoop, calls=%fused_computation.25.clone.clone.clone.clone.clone.clone.2 | loop fusion | flops 47185920 | bytes 5249280 | tf_op jit(solution)/shard_map/kyn,nm->kmy/dot_general | solution.py:169
  149.9 14.7 %broadcast_in_dim.48 = f32[3,1,512,2048]{2,3,0,1:T(8,128)} reshape(f32[3,512,512,4]{1,3,2,0:T(4,128)} %broadcast_in_dim.47) | data formatting | bytes 25165824 | tf_op jit(solution)/shard_map/broadcast_in_dim | solution.py:156
  164.5 17.5 %fusion.36 = bf16[3,1280,512]{2,1,0:T(8,128)(2,1)S(1)} fusion(f32[3,1,512,2048]{2,3,0,1:T(8,128)} %broadcast_in_dim.48, f32[1,1,512,2048]{2,3,0,1:T(8,128)} %get-tuple-element.22, f32[1,1,512,2048]{2,3,0,1:T(8,128)} %get-tuple-element.21, f32[1,1,512,2048]{2,3,0,1:T(8,128)} %get-tuple-element.20, bf16[3,1,512,2048]{2,3,0,1:T(8,128)(2,1)} %copy.30, ...), kind=kOutput, calls=%fused_computation.44 | convolution fusion | flops 8077049856 | bytes 40632320 | tf_op jit(solution)/shard_map/kyn,nm->kmy/dot_general | solution.py:169
  182.0 17.5 %copy.37 = bf16[3,1280,512]{2,0,1:T(4,128)(2,1)} copy(bf16[3,1280,512]{2,1,0:T(8,128)(2,1)S(1)} %fusion.36) | data formatting | bytes 7864320 | tf_op jit(solution)/shard_map/convert_element_type | solution.py:174
  204.6 111.3 %all-to-all-done = bf16[3,1280,512]{2,0,1:T(4,128)(2,1)} async-done(((bf16[3,1280,512]{2,0,1:T(4,128)(2,1)}), bf16[3,1280,512]{2,0,1:T(4,128)(2,1)}, u32[]{:S(2)}, u32[]{:S(2)}) %all-to-all-start) | async-done | bytes 3932192 | tf_op jit(solution)/shard_map/all_to_all | solution.py:175
  324.0 10.0 %reshape.376 = bf16[3,160,2,2048]{3,2,1,0:T(2,128)(2,1)} reshape(bf16[3,320,4,512]{3,2,1,0:T(4,128)(2,1)} %bitcast.237) | data formatting | bytes 7864320 | tf_op jit(solution)/shard_map/reshape | solution.py:103
  334.0 8.6 %fusion.332 = (bf16[3,160,1,2048]{3,2,1,0:T(2,128)(2,1)S(1)}, bf16[3,160,1,2048]{3,2,1,0:T(2,128)(2,1)S(1)}) fusion(bf16[3,160,2,2048]{3,2,1,0:T(2,128)(2,1)} %reshape.376), kind=kLoop, calls=%fused_computation.391 | loop fusion | bytes 7864320 | tf_op jit(solution)/shard_map/slice | solution.py:104
  353.1 8.2 %fusion.163 = f32[256,3,160]{0,2,1:T(8,128)S(1)} fusion(bf16[3,160,2048]{2,1,0:T(8,128)(2,1)S(1)} %get-tuple-element.52, s32[256]{0:T(256)S(1)} %iota_add_fusion.4), kind=kOutput, calls=%fused_computation.180 | convolution fusion | flops 511705088 | bytes 2458624 | tf_op jit(solution)/shard_map/kin,nj->kji/dot_general | solution.py:113
  361.3 8.4 %fusion.159 = f32[256,3,160]{0,2,1:T(8,128)S(1)} fusion(bf16[3,160,2048]{2,1,0:T(8,128)(2,1)S(1)} %get-tuple-element.53, s32[256]{0:T(256)S(1)} %iota_add_fusion.3), kind=kOutput, calls=%fused_computation.179 | convolution fusion | flops 511705088 | bytes 2458624 | tf_op jit(solution)/shard_map/kin,nj->kji/dot_general | solution.py:110
  369.7 8.1 %fusion.157 = f32[256,3,160]{0,2,1:T(8,128)S(1)} fusion(bf16[3,160,2048]{2,1,0:T(8,128)(2,1)S(1)} %get-tuple-element.52, s32[256]{0:T(256)S(1)} %iota_add_fusion.3), kind=kOutput, calls=%fused_computation.178 | convolution fusion | flops 511705088 | bytes 2458624 | tf_op jit(solution)/shard_map/kin,nj->kji/dot_general | solution.py:113
  385.8 8.2 %fusion.151 = f32[256,3,160]{0,2,1:T(8,128)S(1)} fusion(bf16[3,160,2048]{2,1,0:T(8,128)(2,1)S(1)} %get-tuple-element.52, s32[256]{0:T(256)S(1)} %iota_add_fusion.2), kind=kOutput, calls=%fused_computation.176 | convolution fusion | flops 511705088 | bytes 2458624 | tf_op jit(solution)/shard_map/kin,nj->kji/dot_general | solution.py:113
  394.0 8.4 %fusion.147 = f32[256,3,160]{0,2,1:T(8,128)S(1)} fusion(bf16[3,160,2048]{2,1,0:T(8,128)(2,1)S(1)} %get-tuple-element.53, s32[256]{0:T(256)S(1)} %iota_add_fusion.1), kind=kOutput, calls=%fused_computation.175 | convolution fusion | flops 511705088 | bytes 2458624 | tf_op jit(solution)/shard_map/kin,nj->kji/dot_general | solution.py:110
  410.4 8.1 %fusion.141 = f32[256,3,160]{0,2,1:T(8,128)S(1)} fusion(bf16[3,160,2048]{2,1,0:T(8,128)(2,1)S(1)} %get-tuple-element.53, s32[256]{0:T(256)S(1)} %iota_add_fusion), kind=kOutput, calls=%fused_computation.173 | convolution fusion | flops 511705088 | bytes 2458624 | tf_op jit(solution)/shard_map/kin,nj->kji/dot_general | solution.py:110
  418.5 8.2 %fusion.139 = f32[256,3,160]{0,2,1:T(8,128)S(1)} fusion(bf16[3,160,2048]{2,1,0:T(8,128)(2,1)S(1)} %get-tuple-element.52, s32[256]{0:T(256)S(1)} %iota_add_fusion), kind=kOutput, calls=%fused_computation.172 | convolution fusion | flops 511705088 | bytes 2458624 | tf_op jit(solution)/shard_map/kin,nj->kji/dot_general | solution.py:113
  426.7 8.6 %fusion.126 = bf16[3,256,160]{1,2,0:T(8,128)(2,1)S(1)} fusion(f32[256,3,160]{0,2,1:T(8,128)S(1)} %fusion.165, bf16[3,160,2048]{2,1,0:T(8,128)(2,1)S(1)} %get-tuple-element.52, s32[256]{0:T(256)S(1)} %iota_add_fusion.4), kind=kOutput, calls=%fused_computation.160 | convolution fusion | flops 511950848 | bytes 2704384 | tf_op jit(solution)/shard_map/kin,nj->kji/dot_general | solution.py:112
  435.3 8.5 %fusion.125 = bf16[3,256,160]{1,2,0:T(8,128)(2,1)S(1)} fusion(f32[256,3,160]{0,2,1:T(8,128)S(1)} %fusion.163, bf16[3,160,2048]{2,1,0:T(8,128)(2,1)S(1)} %get-tuple-element.53, s32[256]{0:T(256)S(1)} %iota_add_fusion.4), kind=kOutput, calls=%fused_computation.159 | convolution fusion | flops 511950848 | bytes 2704384 | tf_op jit(solution)/shard_map/kin,nj->kji/dot_general | solution.py:115
  443.8 9.0 %fusion.124 = bf16[3,256,160]{1,2,0:T(8,128)(2,1)S(1)} fusion(f32[256,3,160]{0,2,1:T(8,128)S(1)} %fusion.159, bf16[3,160,2048]{2,1,0:T(8,128)(2,1)S(1)} %get-tuple-element.52, s32[256]{0:T(256)S(1)} %iota_add_fusion.3), kind=kOutput, calls=%fused_computation.158 | convolution fusion | flops 511950848 | bytes 2704384 | tf_op jit(solution)/shard_map/kin,nj->kji/dot_general | solution.py:112
  452.8 8.5 %fusion.123 = bf16[3,256,160]{1,2,0:T(8,128)(2,1)S(1)} fusion(f32[256,3,160]{0,2,1:T(8,128)S(1)} %fusion.157, bf16[3,160,2048]{2,1,0:T(8,128)(2,1)S(1)} %get-tuple-element.53, s32[256]{0:T(256)S(1)} %iota_add_fusion.3), kind=kOutput, calls=%fused_computation.157 | convolution fusion | flops 511950848 | bytes 2704384 | tf_op jit(solution)/shard_map/kin,nj->kji/dot_general | solution.py:115
  461.3 8.7 %fusion.122 = bf16[3,256,160]{1,2,0:T(8,128)(2,1)S(1)} fusion(f32[256,3,160]{0,2,1:T(8,128)S(1)} %fusion.153, bf16[3,160,2048]{2,1,0:T(8,128)(2,1)S(1)} %get-tuple-element.52, s32[256]{0:T(256)S(1)} %iota_add_fusion.2), kind=kOutput, calls=%fused_computation.156 | convolution fusion | flops 511950848 | bytes 2704384 | tf_op jit(solution)/shard_map/kin,nj->kji/dot_general | solution.py:112
  470.0 8.5 %fusion.121 = bf16[3,256,160]{1,2,0:T(8,128)(2,1)S(1)} fusion(f32[256,3,160]{0,2,1:T(8,128)S(1)} %fusion.151, bf16[3,160,2048]{2,1,0:T(8,128)(2,1)S(1)} %get-tuple-element.53, s32[256]{0:T(256)S(1)} %iota_add_fusion.2), kind=kOutput, calls=%fused_computation.155 | convolution fusion | flops 511950848 | bytes 2704384 | tf_op jit(solution)/shard_map/kin,nj->kji/dot_general | solution.py:115
  478.5 8.8 %fusion.120 = bf16[3,256,160]{1,2,0:T(8,128)(2,1)S(1)} fusion(f32[256,3,160]{0,2,1:T(8,128)S(1)} %fusion.147, bf16[3,160,2048]{2,1,0:T(8,128)(2,1)S(1)} %get-tuple-element.52, s32[256]{0:T(256)S(1)} %iota_add_fusion.1), kind=kOutput, calls=%fused_computation.154 | convolution fusion | flops 511950848 | bytes 2704384 | tf_op jit(solution)/shard_map/kin,nj->kji/dot_general | solution.py:112
  487.3 8.5 %fusion.119 = bf16[3,256,160]{1,2,0:T(8,128)(2,1)S(1)} fusion(f32[256,3,160]{0,2,1:T(8,128)S(1)} %fusion.145, bf16[3,160,2048]{2,1,0:T(8,128)(2,1)S(1)} %get-tuple-element.53, s32[256]{0:T(256)S(1)} %iota_add_fusion.1), kind=kOutput, calls=%fused_computation.153 | convolution fusion | flops 511950848 | bytes 2704384 | tf_op jit(solution)/shard_map/kin,nj->kji/dot_general | solution.py:115
  495.8 8.8 %fusion.118 = bf16[3,256,160]{1,2,0:T(8,128)(2,1)S(1)} fusion(f32[256,3,160]{0,2,1:T(8,128)S(1)} %fusion.141, bf16[3,160,2048]{2,1,0:T(8,128)(2,1)S(1)} %get-tuple-element.52, s32[256]{0:T(256)S(1)} %iota_add_fusion), kind=kOutput, calls=%fused_computation.152 | convolution fusion | flops 511950848 | bytes 2704384 | tf_op jit(solution)/shard_map/kin,nj->kji/dot_general | solution.py:112
  504.7 8.5 %fusion.117 = bf16[3,256,160]{1,2,0:T(8,128)(2,1)S(1)} fusion(f32[256,3,160]{0,2,1:T(8,128)S(1)} %fusion.139, bf16[3,160,2048]{2,1,0:T(8,128)(2,1)S(1)} %get-tuple-element.53, s32[256]{0:T(256)S(1)} %iota_add_fusion), kind=kOutput, calls=%fused_computation.151 | convolution fusion | flops 511950848 | bytes 2704384 | tf_op jit(solution)/shard_map/kin,nj->kji/dot_general | solution.py:115
  545.9 24.7 %all-to-all-done.1 = bf16[3,1,1280,320]{3,0,1,2:T(4,128)(2,1)} async-done(((bf16[3,1,1280,320]{3,0,1,2:T(4,128)(2,1)}), bf16[3,1,1280,320]{3,0,1,2:T(4,128)(2,1)}, u32[]{:S(2)}, u32[]{:S(2)}) %all-to-all-start.1) | async-done | bytes 2457632 | tf_op jit(solution)/shard_map/all_to_all | solution.py:183
  (77 shorter events, 102.4 us)
Async XLA Ops:
  8.7 123.2 %collective-permute-start = (bf16[3,1,8,512]{3,2,0,1:T(8,128)(2,1)S(1)}, bf16[3,1,8,512]{3,2,0,1:T(8,128)(2,1)S(1)}, u32[]{:S(2)}, u32[]{:S(2)}) collective-permute-start(bf16[3,1,8,512]{3,2,0,1:T(8,128)(2,1)S(1)} %get-tuple-element.25), channel_id=1, source_target_pairs={{0,8},{8,16},{16,24},{24,0},{1,9},{9,17},{17,25},{25,1},{2,10},{10... | collective-permute-start | bytes 73736 | tf_op jit(solution)/shard_map/ppermute | solution.py:28
  11.8 120.1 %collective-permute-start.1 = (bf16[3,1,8,512]{3,2,0,1:T(8,128)(2,1)S(1)}, bf16[3,1,8,512]{3,2,0,1:T(8,128)(2,1)S(1)}, u32[]{:S(2)}, u32[]{:S(2)}) collective-permute-start(bf16[3,1,8,512]{3,2,0,1:T(8,128)(2,1)S(1)} %get-tuple-element.26), channel_id=1, source_target_pairs={{8,0},{16,8},{24,16},{0,24},{9,1},{17,9},{25,17},{1,25},{10,2},{18... | collective-permute-start | bytes 73736 | tf_op jit(solution)/shard_map/ppermute | solution.py:30
  13.9 8.7 %copy-start.5 = (u32[32]{0:T(128)S(1)}, u32[32]{0:T(128)}, u32[]{:S(2)}) copy-start(u32[32]{0:T(128)} %constant.167) | copy-start | bytes 388
  13.9 10.0 %copy-start.2 = (bf16[1,16]{1,0:T(2,128)(2,1)S(1)}, bf16[1,16]{1,0:T(2,128)(2,1)}, u32[]{:S(2)}) copy-start(bf16[1,16]{1,0:T(2,128)(2,1)} %param.9) | copy-start | bytes 100
  13.9 20.6 %copy-start.1 = (bf16[1,16,3072]{2,1,0:T(8,128)(2,1)S(1)}, bf16[1,16,3072]{2,1,0:T(8,128)(2,1)}, u32[]{:S(2)}) copy-start(bf16[1,16,3072]{2,1,0:T(8,128)(2,1)} %param.8) | copy-start | bytes 294916
  66.8 9.7 %copy-start.3 = (s32[1,1,64]{2,1,0:T(1,128)S(1)}, s32[1,1,64]{2,1,0:T(1,128)}, u32[]{:S(2)}) copy-start(s32[1,1,64]{2,1,0:T(1,128)} %param.11) | copy-start | bytes 772
  66.8 9.7 %copy-start.4 = (s32[1,1,64,1]{2,3,1,0:T(1,128)S(1)}, s32[1,1,64,1]{2,3,1,0:T(1,128)}, u32[]{:S(2)}) copy-start(s32[1,1,64,1]{2,3,1,0:T(1,128)} %param.10) | copy-start | bytes 772
  66.8 9.9 %copy-start = (f32[3,1,512,2048]{2,3,0,1:T(8,128)S(1)}, f32[3,1,512,2048]{2,3,0,1:T(8,128)}, u32[]{:S(2)}) copy-start(f32[3,1,512,2048]{2,3,0,1:T(8,128)} %convert_element_type.226) | copy-start | bytes 37748740
  199.5 116.4 %all-to-all-start = ((bf16[3,1280,512]{2,0,1:T(4,128)(2,1)}), bf16[3,1280,512]{2,0,1:T(4,128)(2,1)}, u32[]{:S(2)}, u32[]{:S(2)}) async-start(bf16[3,1280,512]{2,0,1:T(4,128)(2,1)} %copy.37), calls=%async_computation | async-start | bytes 10485760 | tf_op jit(solution)/shard_map/all_to_all | solution.py:175
  519.4 51.1 %all-to-all-start.1 = ((bf16[3,1,1280,320]{3,0,1,2:T(4,128)(2,1)}), bf16[3,1,1280,320]{3,0,1,2:T(4,128)(2,1)}, u32[]{:S(2)}, u32[]{:S(2)}) async-start(bf16[3,1,1280,320]{3,0,1,2:T(4,128)(2,1)} %copy.41), calls=%async_computation.1 | async-start | bytes 7864320 | tf_op jit(solution)/shard_map/all_to_all | solution.py:183
where the time goes:
time: 589 us; the launch traced here: 582 us
  matrix products  200 us (34%)
  waiting for transfers between devices  136 us (23%)
  local copies, waits for them, and re-layouts  111 us (19%)
  other arithmetic  80.1 us (14%)
  blocking collectives  24.9 us (4%)
  between operations  15.4 us (3%)
  starting transfers between devices  15.1 us (3%)
    all_to_all x1, waiting for transfers between devices, per_device(): lax.all_to_all(spectrum, 'row', split_axis=1, concat_axis=2, tiled=True)  111 us
    dot_general x1, other arithmetic, per_device(): jnp.einsum('kyn,nm->kmy', section.reshape(components * depth, rows, point...  45.1 us
    dot_general x5, matrix products, along_y(): jnp.einsum('kin,nj->kji', imag_in, sine, preferred_element_type=jnp.float32)  43.9 us
    dot_general x5, matrix products, along_y(): jnp.einsum('kin,nj->kji', real_in, sine, preferred_element_type=jnp.float32)  42.5 us
    dot_general x5, matrix products, along_y(): jnp.einsum('kin,nj->kji', real_in, cosine, preferred_element_type=jnp.flo...  40.9 us
    dot_general x5, matrix products, along_y(): jnp.einsum('kin,nj->kji', imag_in, cosine, preferred_element_type=jnp.flo...  40.7 us
    broadcast_in_dim x5, local copies, waits for them, and re-layouts, per_device(): forcing = jnp.repeat(jnp.repeat(coarse, RATIO, axis=2), RATIO, axis=3)  30.2 us
    all_to_all x1, waiting for transfers between devices, per_device(): lax.all_to_all(ordered, 'col', split_axis=2, concat_axis=1, tiled=True)  24.7 us
  transfers between devices with their start and end apart: 4, of which 2 were waited for; matrix products, arithmetic and copies ran while one was open for 17% of the time, Pallas kernels for 0%

commit v1 on v0

--- a/solution.py
+++ b/solution.py
@@ -3,6 +3,7 @@
 import jax.numpy as jnp
 from jax import lax
 from jax.sharding import PartitionSpec as P
+from jax.lax import all_to_all, axis_size
 
 NX = 2048
 NY = 2048
@@ -172,7 +173,16 @@
         xtable,
         preferred_element_type=jnp.float32,
     ).astype(jnp.bfloat16)
-    ordered = along_y(lax.all_to_all(spectrum, "row", split_axis=1, concat_axis=2, tiled=True))
+
+    def shape_body(mine_x):
+        right_arr = axis_size("row")
+        taken_in = jnp.split(mine_x, right_arr, 1)
+        o_now = jnp.stack(taken_in, axis=0)
+        even = all_to_all(o_now, "row", 0, 0)
+        current_arr = jnp.concatenate(even, 2)
+        return current_arr
+
+    ordered = along_y(shape_body(spectrum))
     ordered = ordered.reshape(components, depth, KYM, -1)
     inverse = vertical_inverse(depth * lax.axis_size("col")).astype(jnp.bfloat16)
     mode_rows = KYM // lax.axis_size("col")

time: 589 us -> 544 us (0.924)
  waiting for transfers between devices: 136 us -> 108 us
  local copies, waits for them, and re-layouts: 111 us -> 92.6 us
    all_to_all x1, waiting for transfers between devices: 111 us -> 83.2 us  [shape_body(): even = all_to_all(o_now, 'row', 0, 0)]
    convert_element_type x1 -> x0, local copies, waits for them, and re-layouts: 17.5 us -> none  [per_device(): spectrum = jnp.einsum('kyn,nm->kmy', section.reshape(components * depth,...]
    another operation x0 -> x2, local copies, waits for them, and re-layouts: none -> 10.5 us  [the longest x1 9.99 us: along_y(): split = piece.reshape(items, half, 2, length)]
    all_to_all x1 -> x0, local copies, waits for them, and re-layouts: 8.12 us -> none  [per_device(): lax.all_to_all(spectrum, 'row', split_axis=1, concat_axis=2, tiled=True)]
  transfers between devices with their start and end apart: 4 -> 4, of which waited for: 2 -> 2; matrix products, arithmetic and copies ran while one was open for 17% -> 19% of each run, Pallas kernels for 0% -> 0%
where the time goes in v1:
time: 544 us; the launch traced here: 538 us
  matrix products  200 us (37%)
  waiting for transfers between devices  108 us (20%)
  local copies, waits for them, and re-layouts  92.6 us (17%)
  other arithmetic  82.3 us (15%)
  blocking collectives  24.9 us (5%)
  between operations  15.5 us (3%)
  starting transfers between devices  14.8 us (3%)
    all_to_all x1, waiting for transfers between devices, shape_body(): even = all_to_all(o_now, 'row', 0, 0)  83.2 us
    dot_general x1, other arithmetic, per_device(): jnp.einsum('kyn,nm->kmy', section.reshape(components * depth, rows, point...  45.1 us
    dot_general x5, matrix products, along_y(): jnp.einsum('kin,nj->kji', imag_in, sine, preferred_element_type=jnp.float32)  43.9 us
    dot_general x5, matrix products, along_y(): jnp.einsum('kin,nj->kji', real_in, sine, preferred_element_type=jnp.float32)  42.5 us
    dot_general x5, matrix products, along_y(): jnp.einsum('kin,nj->kji', real_in, cosine, preferred_element_type=jnp.flo...  40.9 us
    dot_general x5, matrix products, along_y(): jnp.einsum('kin,nj->kji', imag_in, cosine, preferred_element_type=jnp.flo...  40.7 us
    broadcast_in_dim x5, local copies, waits for them, and re-layouts, per_device(): forcing = jnp.repeat(jnp.repeat(coarse, RATIO, axis=2), RATIO, axis=3)  30.2 us
    all_to_all x1, waiting for transfers between devices, per_device(): lax.all_to_all(ordered, 'col', split_axis=2, concat_axis=1, tiled=True)  24.6 us
  transfers between devices with their start and end apart: 4, of which 2 were waited for; matrix products, arithmetic and copies ran while one was open for 19% of the time, Pallas kernels for 0%

profile of v1, /device:TPU:0, one launch (start us, length us, event | category | flops | bytes accessed | tf_op | source)
XLA Modules:
  0.0 537.9 jit_solution(12512847664156099405)
XLA Ops:
  13.9 8.7 %copy.30 = bf16[3,1,512,2048]{2,3,0,1:T(8,128)(2,1)} copy(bf16[3,1,512,2048]{3,2,1,0:T(8,128)(2,1)} %param.6) | data formatting | bytes 12582912 | tf_op args[0]
  24.1 10.3 %all-reduce = bf16[64]{0:T(256)(128)(2,1)S(1)} all-reduce(bf16[64]{0:T(256)(128)(2,1)S(1)} %dynamic-update-slice), channel_id=1, replica_groups=mesh['row'=4,'col'=8] {'row'}, use_global_device_ids=true, to_apply=%add | all-reduce | flops 64 | bytes 256 | tf_op jit(solution)/shard_map/reshape
  34.4 14.6 %all_gather.7 = bf16[1,64,3072]{2,1,0:T(8,128)(2,1)S(1)} all-gather(bf16[1,16,3072]{2,1,0:T(8,128)(2,1)S(1)} %copy-done.1), channel_id=1, replica_groups=mesh['row'=4,'col'=8] {'row'}, dimensions={1}, use_global_device_ids=true | all-gather | bytes 491520 | tf_op jit(solution)/shard_map/all_gather | solution.py:143
  49.0 9.2 %convert_element_type.226 = f32[3,1,512,2048]{2,3,0,1:T(8,128)} convert(bf16[3,1,512,2048]{2,3,0,1:T(8,128)(2,1)} %copy.30) | non-fusion elementwise | flops 3145728 | bytes 18874368 | tf_op jit(solution)/shard_map/convert_element_type | solution.py:158
  58.2 8.6 %copy.31 = bf16[3,1,512,2048]{2,3,0,1:T(8,128)(2,1)} copy(bf16[3,1,512,2048]{3,2,1,0:T(8,128)(2,1)} %param.7) | data formatting | bytes 12582912 | tf_op args[1]
  66.8 9.7 %convert_element_type.227 = f32[3,1,512,2048]{2,3,0,1:T(8,128)} convert(bf16[3,1,512,2048]{2,3,0,1:T(8,128)(2,1)} %copy.31) | non-fusion elementwise | flops 3145728 | bytes 18874368 | tf_op jit(solution)/shard_map/convert_element_type | solution.py:159
  76.8 10.0 %multiply_subtract_fusion.2 = (f32[1,1,512,2048]{2,3,0,1:T(8,128)}, f32[1,1,512,2048]{2,3,0,1:T(8,128)}, f32[1,1,512,2048]{2,3,0,1:T(8,128)}) fusion(f32[3,1,512,2048]{2,3,0,1:T(8,128)} %convert_element_type.227, f32[3,1,512,2048]{2,3,0,1:T(8,128)S(1)} %copy-done), kind=kLoop, calls=%fused_computation.41 | loop fusion | flops 9437184 | bytes 37748736 | tf_op jit(solution)/shard_map/sub | solution.py:162
  86.8 45.1 %fusion.364 = bf16[2048,1280,1]{0,1,2:T(8,128)(2,1)} fusion(s32[1280]{0:T(1024)S(1)} %add_select_fusion.7, pred[1280]{0:T(1024)(128)(4,1)S(1)} %fusion.192), kind=kLoop, calls=%fused_computation.25.clone.clone.clone.clone.clone.clone.2 | loop fusion | flops 47185920 | bytes 5249280 | tf_op jit(solution)/shard_map/kyn,nm->kmy/dot_general | solution.py:170
  149.9 14.7 %broadcast_in_dim.48 = f32[3,1,512,2048]{2,3,0,1:T(8,128)} reshape(f32[3,512,512,4]{1,3,2,0:T(4,128)} %broadcast_in_dim.47) | data formatting | bytes 25165824 | tf_op jit(solution)/shard_map/broadcast_in_dim | solution.py:157
  164.5 17.4 %fusion.36 = bf16[3,1280,512]{2,1,0:T(8,128)(2,1)S(1)} fusion(f32[3,1,512,2048]{2,3,0,1:T(8,128)} %broadcast_in_dim.48, f32[1,1,512,2048]{2,3,0,1:T(8,128)} %get-tuple-element.22, f32[1,1,512,2048]{2,3,0,1:T(8,128)} %get-tuple-element.21, f32[1,1,512,2048]{2,3,0,1:T(8,128)} %get-tuple-element.20, bf16[3,1,512,2048]{2,3,0,1:T(8,128)(2,1)} %copy.30, ...), kind=kOutput, calls=%fused_computation.44 | convolution fusion | flops 8077049856 | bytes 40632320 | tf_op jit(solution)/shard_map/kyn,nm->kmy/dot_general | solution.py:170
  189.5 83.2 %all-to-all-done = bf16[4,3,320,512]{3,2,1,0:T(8,128)(2,1)} async-done(((bf16[4,3,320,512]{3,2,1,0:T(8,128)(2,1)}), bf16[4,3,320,512]{3,2,1,0:T(8,128)(2,1)}, u32[]{:S(2)}, u32[]{:S(2)}) %all-to-all-start) | async-done | bytes 3932192 | tf_op jit(solution)/shard_map/all_to_all | solution.py:181
  279.8 10.0 %reshape_reshape.3 = bf16[3,160,2,2048]{3,2,1,0:T(2,128)(2,1)} reshape(bf16[3,320,4,512]{3,2,1,0:T(4,128)(2,1)} %copy.37) | data formatting | bytes 7864320 | tf_op jit(solution)/shard_map/reshape;reshape | solution.py:104
  289.8 8.5 %fusion.332 = (bf16[3,160,1,2048]{3,2,1,0:T(2,128)(2,1)S(1)}, bf16[3,160,1,2048]{3,2,1,0:T(2,128)(2,1)S(1)}) fusion(bf16[3,160,2,2048]{3,2,1,0:T(2,128)(2,1)} %reshape_reshape.3), kind=kLoop, calls=%fused_computation.395 | loop fusion | bytes 7864320 | tf_op jit(solution)/shard_map/slice | solution.py:105
  308.8 8.2 %fusion.139 = f32[256,3,160]{0,2,1:T(8,128)S(1)} fusion(bf16[3,160,2048]{2,1,0:T(8,128)(2,1)S(1)} %get-tuple-element.56, s32[256]{0:T(256)S(1)} %iota_add_fusion), kind=kOutput, calls=%fused_computation.172 | convolution fusion | flops 511705088 | bytes 2458624 | tf_op jit(solution)/shard_map/kin,nj->kji/dot_general | solution.py:114
  317.0 8.4 %fusion.147 = f32[256,3,160]{0,2,1:T(8,128)S(1)} fusion(bf16[3,160,2048]{2,1,0:T(8,128)(2,1)S(1)} %get-tuple-element.57, s32[256]{0:T(256)S(1)} %iota_add_fusion.1), kind=kOutput, calls=%fused_computation.175 | convolution fusion | flops 511705088 | bytes 2458624 | tf_op jit(solution)/shard_map/kin,nj->kji/dot_general | solution.py:111
  325.4 8.1 %fusion.145 = f32[256,3,160]{0,2,1:T(8,128)S(1)} fusion(bf16[3,160,2048]{2,1,0:T(8,128)(2,1)S(1)} %get-tuple-element.56, s32[256]{0:T(256)S(1)} %iota_add_fusion.1), kind=kOutput, calls=%fused_computation.174 | convolution fusion | flops 511705088 | bytes 2458624 | tf_op jit(solution)/shard_map/kin,nj->kji/dot_general | solution.py:114
  333.5 8.0 %fusion.153 = f32[256,3,160]{0,2,1:T(8,128)S(1)} fusion(bf16[3,160,2048]{2,1,0:T(8,128)(2,1)S(1)} %get-tuple-element.57, s32[256]{0:T(256)S(1)} %iota_add_fusion.2), kind=kOutput, calls=%fused_computation.177 | convolution fusion | flops 511705088 | bytes 2458624 | tf_op jit(solution)/shard_map/kin,nj->kji/dot_general | solution.py:111
  341.5 8.2 %fusion.151 = f32[256,3,160]{0,2,1:T(8,128)S(1)} fusion(bf16[3,160,2048]{2,1,0:T(8,128)(2,1)S(1)} %get-tuple-element.56, s32[256]{0:T(256)S(1)} %iota_add_fusion.2), kind=kOutput, calls=%fused_computation.176 | convolution fusion | flops 511705088 | bytes 2458624 | tf_op jit(solution)/shard_map/kin,nj->kji/dot_general | solution.py:114
  349.7 8.4 %fusion.159 = f32[256,3,160]{0,2,1:T(8,128)S(1)} fusion(bf16[3,160,2048]{2,1,0:T(8,128)(2,1)S(1)} %get-tuple-element.57, s32[256]{0:T(256)S(1)} %iota_add_fusion.3), kind=kOutput, calls=%fused_computation.179 | convolution fusion | flops 511705088 | bytes 2458624 | tf_op jit(solution)/shard_map/kin,nj->kji/dot_general | solution.py:111
  366.1 8.1 %fusion.165 = f32[256,3,160]{0,2,1:T(8,128)S(1)} fusion(bf16[3,160,2048]{2,1,0:T(8,128)(2,1)S(1)} %get-tuple-element.57, s32[256]{0:T(256)S(1)} %iota_add_fusion.4), kind=kOutput, calls=%fused_computation.181 | convolution fusion | flops 511705088 | bytes 2458624 | tf_op jit(solution)/shard_map/kin,nj->kji/dot_general | solution.py:111
  374.2 8.2 %fusion.163 = f32[256,3,160]{0,2,1:T(8,128)S(1)} fusion(bf16[3,160,2048]{2,1,0:T(8,128)(2,1)S(1)} %get-tuple-element.56, s32[256]{0:T(256)S(1)} %iota_add_fusion.4), kind=kOutput, calls=%fused_computation.180 | convolution fusion | flops 511705088 | bytes 2458624 | tf_op jit(solution)/shard_map/kin,nj->kji/dot_general | solution.py:114
  382.4 8.6 %fusion.118 = bf16[3,256,160]{1,2,0:T(8,128)(2,1)S(1)} fusion(f32[256,3,160]{0,2,1:T(8,128)S(1)} %fusion.141, bf16[3,160,2048]{2,1,0:T(8,128)(2,1)S(1)} %get-tuple-element.56, s32[256]{0:T(256)S(1)} %iota_add_fusion), kind=kOutput, calls=%fused_computation.152 | convolution fusion | flops 511950848 | bytes 2704384 | tf_op jit(solution)/shard_map/kin,nj->kji/dot_general | solution.py:113
  391.0 8.5 %fusion.117 = bf16[3,256,160]{1,2,0:T(8,128)(2,1)S(1)} fusion(f32[256,3,160]{0,2,1:T(8,128)S(1)} %fusion.139, bf16[3,160,2048]{2,1,0:T(8,128)(2,1)S(1)} %get-tuple-element.57, s32[256]{0:T(256)S(1)} %iota_add_fusion), kind=kOutput, calls=%fused_computation.151 | convolution fusion | flops 511950848 | bytes 2704384 | tf_op jit(solution)/shard_map/kin,nj->kji/dot_general | solution.py:116
  399.5 9.0 %fusion.120 = bf16[3,256,160]{1,2,0:T(8,128)(2,1)S(1)} fusion(f32[256,3,160]{0,2,1:T(8,128)S(1)} %fusion.147, bf16[3,160,2048]{2,1,0:T(8,128)(2,1)S(1)} %get-tuple-element.56, s32[256]{0:T(256)S(1)} %iota_add_fusion.1), kind=kOutput, calls=%fused_computation.154 | convolution fusion | flops 511950848 | bytes 2704384 | tf_op jit(solution)/shard_map/kin,nj->kji/dot_general | solution.py:113
  408.5 8.5 %fusion.119 = bf16[3,256,160]{1,2,0:T(8,128)(2,1)S(1)} fusion(f32[256,3,160]{0,2,1:T(8,128)S(1)} %fusion.145, bf16[3,160,2048]{2,1,0:T(8,128)(2,1)S(1)} %get-tuple-element.57, s32[256]{0:T(256)S(1)} %iota_add_fusion.1), kind=kOutput, calls=%fused_computation.153 | convolution fusion | flops 511950848 | bytes 2704384 | tf_op jit(solution)/shard_map/kin,nj->kji/dot_general | solution.py:116
  417.0 8.7 %fusion.122 = bf16[3,256,160]{1,2,0:T(8,128)(2,1)S(1)} fusion(f32[256,3,160]{0,2,1:T(8,128)S(1)} %fusion.153, bf16[3,160,2048]{2,1,0:T(8,128)(2,1)S(1)} %get-tuple-element.56, s32[256]{0:T(256)S(1)} %iota_add_fusion.2), kind=kOutput, calls=%fused_computation.156 | convolution fusion | flops 511950848 | bytes 2704384 | tf_op jit(solution)/shard_map/kin,nj->kji/dot_general | solution.py:113
  425.7 8.5 %fusion.121 = bf16[3,256,160]{1,2,0:T(8,128)(2,1)S(1)} fusion(f32[256,3,160]{0,2,1:T(8,128)S(1)} %fusion.151, bf16[3,160,2048]{2,1,0:T(8,128)(2,1)S(1)} %get-tuple-element.57, s32[256]{0:T(256)S(1)} %iota_add_fusion.2), kind=kOutput, calls=%fused_computation.155 | convolution fusion | flops 511950848 | bytes 2704384 | tf_op jit(solution)/shard_map/kin,nj->kji/dot_general | solution.py:116
  434.2 8.8 %fusion.124 = bf16[3,256,160]{1,2,0:T(8,128)(2,1)S(1)} fusion(f32[256,3,160]{0,2,1:T(8,128)S(1)} %fusion.159, bf16[3,160,2048]{2,1,0:T(8,128)(2,1)S(1)} %get-tuple-element.56, s32[256]{0:T(256)S(1)} %iota_add_fusion.3), kind=kOutput, calls=%fused_computation.158 | convolution fusion | flops 511950848 | bytes 2704384 | tf_op jit(solution)/shard_map/kin,nj->kji/dot_general | solution.py:113
  443.0 8.5 %fusion.123 = bf16[3,256,160]{1,2,0:T(8,128)(2,1)S(1)} fusion(f32[256,3,160]{0,2,1:T(8,128)S(1)} %fusion.157, bf16[3,160,2048]{2,1,0:T(8,128)(2,1)S(1)} %get-tuple-element.57, s32[256]{0:T(256)S(1)} %iota_add_fusion.3), kind=kOutput, calls=%fused_computation.157 | convolution fusion | flops 511950848 | bytes 2704384 | tf_op jit(solution)/shard_map/kin,nj->kji/dot_general | solution.py:116
  451.5 8.8 %fusion.126 = bf16[3,256,160]{1,2,0:T(8,128)(2,1)S(1)} fusion(f32[256,3,160]{0,2,1:T(8,128)S(1)} %fusion.165, bf16[3,160,2048]{2,1,0:T(8,128)(2,1)S(1)} %get-tuple-element.56, s32[256]{0:T(256)S(1)} %iota_add_fusion.4), kind=kOutput, calls=%fused_computation.160 | convolution fusion | flops 511950848 | bytes 2704384 | tf_op jit(solution)/shard_map/kin,nj->kji/dot_general | solution.py:113
  460.4 8.5 %fusion.125 = bf16[3,256,160]{1,2,0:T(8,128)(2,1)S(1)} fusion(f32[256,3,160]{0,2,1:T(8,128)S(1)} %fusion.163, bf16[3,160,2048]{2,1,0:T(8,128)(2,1)S(1)} %get-tuple-element.57, s32[256]{0:T(256)S(1)} %iota_add_fusion.4), kind=kOutput, calls=%fused_computation.159 | convolution fusion | flops 511950848 | bytes 2704384 | tf_op jit(solution)/shard_map/kin,nj->kji/dot_general | solution.py:116
  501.7 24.6 %all-to-all-done.1 = bf16[3,1,1280,320]{3,0,1,2:T(4,128)(2,1)} async-done(((bf16[3,1,1280,320]{3,0,1,2:T(4,128)(2,1)}), bf16[3,1,1280,320]{3,0,1,2:T(4,128)(2,1)}, u32[]{:S(2)}, u32[]{:S(2)}) %all-to-all-start.1) | async-done | bytes 2457632 | tf_op jit(solution)/shard_map/all_to_all | solution.py:193
  (78 shorter events, 95.8 us)
Async XLA Ops:
  8.7 123.2 %collective-permute-start = (bf16[3,1,8,512]{3,2,0,1:T(8,128)(2,1)S(1)}, bf16[3,1,8,512]{3,2,0,1:T(8,128)(2,1)S(1)}, u32[]{:S(2)}, u32[]{:S(2)}) collective-permute-start(bf16[3,1,8,512]{3,2,0,1:T(8,128)(2,1)S(1)} %get-tuple-element.29), channel_id=1, source_target_pairs={{0,8},{8,16},{16,24},{24,0},{1,9},{9,17},{17,25},{25,1},{2,10},{10... | collective-permute-start | bytes 73736 | tf_op jit(solution)/shard_map/ppermute | solution.py:29
  11.8 120.1 %collective-permute-start.1 = (bf16[3,1,8,512]{3,2,0,1:T(8,128)(2,1)S(1)}, bf16[3,1,8,512]{3,2,0,1:T(8,128)(2,1)S(1)}, u32[]{:S(2)}, u32[]{:S(2)}) collective-permute-start(bf16[3,1,8,512]{3,2,0,1:T(8,128)(2,1)S(1)} %get-tuple-element.30), channel_id=1, source_target_pairs={{8,0},{16,8},{24,16},{0,24},{9,1},{17,9},{25,17},{1,25},{10,2},{18... | collective-permute-start | bytes 73736 | tf_op jit(solution)/shard_map/ppermute | solution.py:31
  13.9 8.7 %copy-start.5 = (u32[32]{0:T(128)S(1)}, u32[32]{0:T(128)}, u32[]{:S(2)}) copy-start(u32[32]{0:T(128)} %constant.167) | copy-start | bytes 388
  13.9 10.0 %copy-start.2 = (bf16[1,16]{1,0:T(2,128)(2,1)S(1)}, bf16[1,16]{1,0:T(2,128)(2,1)}, u32[]{:S(2)}) copy-start(bf16[1,16]{1,0:T(2,128)(2,1)} %param.9) | copy-start | bytes 100
  13.9 20.5 %copy-start.1 = (bf16[1,16,3072]{2,1,0:T(8,128)(2,1)S(1)}, bf16[1,16,3072]{2,1,0:T(8,128)(2,1)}, u32[]{:S(2)}) copy-start(bf16[1,16,3072]{2,1,0:T(8,128)(2,1)} %param.8) | copy-start | bytes 294916
  66.8 9.7 %copy-start.3 = (s32[1,1,64]{2,1,0:T(1,128)S(1)}, s32[1,1,64]{2,1,0:T(1,128)}, u32[]{:S(2)}) copy-start(s32[1,1,64]{2,1,0:T(1,128)} %param.11) | copy-start | bytes 772
  66.8 9.7 %copy-start.4 = (s32[1,1,64,1]{2,3,1,0:T(1,128)S(1)}, s32[1,1,64,1]{2,3,1,0:T(1,128)}, u32[]{:S(2)}) copy-start(s32[1,1,64,1]{2,3,1,0:T(1,128)} %param.10) | copy-start | bytes 772
  66.8 9.9 %copy-start = (f32[3,1,512,2048]{2,3,0,1:T(8,128)S(1)}, f32[3,1,512,2048]{2,3,0,1:T(8,128)}, u32[]{:S(2)}) copy-start(f32[3,1,512,2048]{2,3,0,1:T(8,128)} %convert_element_type.226) | copy-start | bytes 37748740
  184.6 88.1 %all-to-all-start = ((bf16[4,3,320,512]{3,2,1,0:T(8,128)(2,1)}), bf16[4,3,320,512]{3,2,1,0:T(8,128)(2,1)}, u32[]{:S(2)}, u32[]{:S(2)}) async-start(bf16[4,3,320,512]{3,2,1,0:T(8,128)(2,1)} %pad_maximum_fusion), calls=%async_computation | async-start | bytes 7864320 | tf_op jit(solution)/shard_map/all_to_all | solution.py:181
  475.1 51.1 %all-to-all-start.1 = ((bf16[3,1,1280,320]{3,0,1,2:T(4,128)(2,1)}), bf16[3,1,1280,320]{3,0,1,2:T(4,128)(2,1)}, u32[]{:S(2)}, u32[]{:S(2)}) async-start(bf16[3,1,1280,320]{3,0,1,2:T(4,128)(2,1)} %copy.40), calls=%async_computation.1 | async-start | bytes 7864320 | tf_op jit(solution)/shard_map/all_to_all | solution.py:193
